TPU v7x, 32 devices: a whole 2x2x4 slice. The times are simulated.
32 devices in a mesh: prow: 8 (over z, y), pcol: 4 (over x, core).
Axes of the slice: x: 2, y: 2, z: 4, core: 2. Of those that a mesh axis runs over, the one named last changes fastest.
Arguments:
- paper_x: bfloat16 [8192, 768], P(('prow', 'pcol')), may hold values from -6 to 6
- author_x: bfloat16 [4096, 768], P(('pcol', 'prow')), may hold values from -6 to 6
- w_self: bfloat16 [768, 768], replicated, may hold values from -0.21875 to 0.21875
- w_rel: bfloat16 [2, 768, 768], replicated, may hold values from -0.009765625 to 0.009765625
- w_two: bfloat16 [768, 768], replicated, may hold values from -0.0068359375 to 0.0068359375
- block_rows: int32 [8, 4, 32], P('prow', 'pcol'), may hold values from 0 to 7, as said below
- block_cols: int32 [8, 4, 32], P('prow', 'pcol'), may hold values from 0 to 7, as said below
- block_type: int32 [8, 4, 32], P('prow', 'pcol'), may hold values from 0 to 1
- block_count: int32 [8, 4], P('prow', 'pcol'), may hold values from 8 to 32, as said below
- block_vals: bfloat16 [8, 4, 32, 128, 128], P('prow', 'pcol'), may hold values from 0 to 1, as said below
Outputs:
- paper_hidden: bfloat16 [8192, 768], P(('prow', 'pcol'))
- author_out: bfloat16 [4096, 768], P(('pcol', 'prow'))
Inputs may be any that keep to these rules, and one draw needn't show every extreme that they name: `block_rows`: within one tile the live and dead slots name distinct positions; block rows are below 8. `block_cols`: block columns are below 8; with block_rows, positions of one tile are distinct. `block_count`: slots 0 to count - 1 of a tile are live; some tile holds 32 live slots and some tile 32 // 4 in every draw. `block_vals`: every entry is 0 or 1.
All inputs are finite; a program needn't handle non-finite values.
Results may differ from a plain program's by a relative error of at most 0.0041.
Values may be sent and summed in bfloat16 or wider, within the bound.
A program may use at most 64 MiB of HBM per device.

v0:
```python
import jax
import jax.numpy as jnp
from jax import lax
from jax.sharding import PartitionSpec as P

GROUP = 16


def per_device(
    paper_x,
    author_x,
    w_self,
    w_rel,
    w_two,
    block_rows,
    block_cols,
    block_type,
    block_count,
    block_vals,
):
    slots = block_rows.shape[2]
    side = block_vals.shape[3]
    width = paper_x.shape[1]
    relations = w_rel.shape[0]
    groups = slots // GROUP
    own_rows = paper_x.shape[0]
    row_ids = block_rows.reshape(groups, GROUP)
    col_ids = block_cols.reshape(groups, GROUP)
    type_ids = block_type.reshape(groups, GROUP)
    live = (
        (jnp.arange(slots, dtype=jnp.int32) < block_count.reshape(()))
        .astype(jnp.float32)
        .reshape(groups, GROUP)
    )
    contents = block_vals.reshape(groups, GROUP, side, side)
    self_term = jnp.dot(paper_x, w_self, preferred_element_type=jnp.float32)
    authors = lax.all_gather(author_x, "prow", axis=0, tiled=True)
    messages = jnp.stack(
        [
            jnp.dot(authors, w_rel[index], preferred_element_type=jnp.float32)
            for index in range(relations)
        ]
    ).astype(jnp.bfloat16)
    col_blocks = messages.shape[1] // side
    row_blocks = own_rows * lax.axis_size("pcol") // side
    table = messages.reshape(relations * col_blocks, side, width)
    row_range = jnp.arange(row_blocks, dtype=jnp.int32)
    col_range = jnp.arange(col_blocks, dtype=jnp.int32)

    def first_hop(total, item):
        rows_now, cols_now, types_now, mask_now, content_now = item
        picked = table[types_now * col_blocks + cols_now]
        product = jnp.einsum(
            "kpa,kaf->kpf", content_now, picked, preferred_element_type=jnp.float32
        )
        placing = (rows_now[:, None] == row_range[None, :]).astype(jnp.float32) * mask_now[:, None]
        return (
            total + jnp.einsum("kr,kpf->rpf", placing, product, precision=lax.Precision.HIGHEST),
            None,
        )

    start = jnp.zeros((row_blocks, side, width), jnp.float32)
    partial_value, _ = lax.scan(first_hop, start, (row_ids, col_ids, type_ids, live, contents))
    partial_value = partial_value.reshape(row_blocks * side, width)
    summed = lax.psum_scatter(partial_value, "pcol", scatter_dimension=0, tiled=True)
    paper_hidden = jnp.maximum(self_term + summed, 0.0).astype(jnp.bfloat16)
    outgoing = jnp.dot(paper_hidden, w_two, preferred_element_type=jnp.float32).astype(jnp.bfloat16)
    paper_rows = lax.all_gather(outgoing, "pcol", axis=0, tiled=True).reshape(
        row_blocks, side, width
    )

    def second_hop(total, item):
        rows_now, cols_now, mask_now, content_now = item
        picked = paper_rows[rows_now]
        product = jnp.einsum(
            "kpa,kpf->kaf", content_now, picked, preferred_element_type=jnp.float32
        )
        placing = (cols_now[:, None] == col_range[None, :]).astype(jnp.float32) * mask_now[:, None]
        return (
            total + jnp.einsum("kc,kaf->caf", placing, product, precision=lax.Precision.HIGHEST),
            None,
        )

    start_two = jnp.zeros((col_blocks, side, width), jnp.float32)
    author_part, _ = lax.scan(second_hop, start_two, (row_ids, col_ids, live, contents))
    author_total = lax.psum_scatter(
        author_part.reshape(col_blocks * side, width), "prow", scatter_dimension=0, tiled=True
    )
    return (paper_hidden, author_total.astype(jnp.bfloat16))


def solution(mesh):
    return jax.shard_map(
        per_device,
        mesh=mesh,
        in_specs=(
            P(("prow", "pcol"), None),
            P(("pcol", "prow"), None),
            P(),
            P(),
            P(),
            P("prow", "pcol", None),
            P("prow", "pcol", None),
            P("prow", "pcol", None),
            P("prow", "pcol"),
            P("prow", "pcol", None, None, None),
        ),
        out_specs=(P(("prow", "pcol"), None), P(("pcol", "prow"), None)),
        check_vma=False,
    )
```

profile of v0, /device:TPU:0, one launch (start us, length us, event | category | flops | bytes accessed | tf_op | source)
XLA Modules:
  0.0 299.5 jit_solution(3397042512454895330)
XLA Ops:
  7.2 0.0 copy-start
  7.2 0.0 all-gather.3.cloned.1.call-start
  7.2 0.7 all-gather.3.cloned.1.call-update
  7.9 0.0 reduce-scatter.3.cloned.1.call-start
  8.0 0.5 broadcast.116
  8.5 1.3 reduce.9
  9.8 0.1 reshape.103
  9.9 1.3 reduce.11
  11.2 0.1 reshape.107
  11.3 1.3 reduce.10
  12.6 0.1 reshape.106
  13.4 43.8 %all-gather.3.cloned.1.call-done = bf16[1024,768]{1,0:T(8,128)(2,1)} async-done(((bf16[128,768]{1,0:T(8,128)(2,1)}), bf16[1024,768]{1,0:T(8,128)(2,1)}) %all-gather.3.cloned.1.call-update) | async-done | bytes 1572880 | tf_op jit(solution)/shard_map/all_gather | solution.py:37
  57.1 3.3 %fusion.41 = bf16[1,1024,768]{2,1,0:T(8,128)(2,1)S(1)} fusion(bf16[1024,768]{1,0:T(8,128)(2,1)} %all-gather.3.cloned.1.call-done, bf16[2,768,768]{2,1,0:T(8,128)(2,1)} %param.17), kind=kOutput, calls=%fused_computation.55 | convolution fusion | flops 1208745984 | bytes 4325376 | tf_op jit(solution)/shard_map/dot_general | solution.py:40
  60.4 0.0 copy-done.4
  60.4 0.0 copy-done.5
  60.4 1.4 fusion.42
  61.8 0.0 copy-start.1
  61.8 2.0 pad_maximum_fusion
  63.8 0.0 copy-done.1
  63.8 41.9 %while.22 = (s32[]{:T(128)}, f32[8,128,768]{2,0,1:T(8,128)}, s32[2,16]{1,0:T(2,128)S(1)}, f32[2,16]{1,0:T(2,128)S(1)}, bf16[2,16,128,128]{3,2,1,0:T(8,128)(2,1)S...) while((s32[]{:T(128)}, f32[8,128,768]{2,0,1:T(8,128)}, ...), condition=%wide.region_1.2_spmd.clone, body=%wide.region_0.1_spmd.clone.sunk | while | flops 555222400 | bytes 28840768 | solution.py:63
  63.8 4.3 %gather_fusion = bf16[16,128,768]{2,1,0:T(8,128)(2,1)} fusion(bf16[16,128,768]{2,1,0:T(8,128)(2,1)} %get-tuple-element.297, s32[1024]{0:T(1024)S(1)} %pad_clamp_fusion.4), kind=kCustom, calls=%fused_computation.clone.clone.1 | custom fusion | bytes 6291520 | tf_op jit(solution)/shard_map/while/body/eval_jaxpr/gather | solution.py:52
  68.1 5.5 %fusion.78 = f32[16,128,768]{2,1,0:T(8,128)} fusion(bf16[16,128,768]{2,1,0:T(8,128)(2,1)} %gather_fusion, bf16[2,16,128,128]{3,2,1,0:T(8,128)(2,1)S(1)} %get-tuple-element.294, s32[]{:T(128)} %get-tuple-element.280), kind=kOutput, calls=%fused_computation.7.clone.1 | convolution fusion | flops 402653184 | bytes 9961476 | tf_op jit(solution)/shard_map/while/body/eval_jaxpr/kpa,kaf->kpf/dot_general | solution.py:53
  73.6 10.9 %select_add_fusion.4 = f32[8,128,768]{2,0,1:T(8,128)} fusion(f32[8,128,768]{2,0,1:T(8,128)} %get-tuple-element.281, f32[16,128,768]{2,1,0:T(8,128)} %fusion.78, pred[]{:T(512)S(6)} %compare.6, f32[16]{0:T(128)S(1)} %fusion.79, s32[16]{0:T(128)S(1)} %fusion.80), kind=kOutput, calls=%fused_computation.6.clone.1 | convolution fusion | flops 152568064 | bytes 12583041 | tf_op jit(solution)/shard_map/while/body/eval_jaxpr/kr,kpf->rpf/dot_general | solution.py:58
  84.5 4.3 %gather_fusion = bf16[16,128,768]{2,1,0:T(8,128)(2,1)} fusion(bf16[16,128,768]{2,1,0:T(8,128)(2,1)} %get-tuple-element.297, s32[1024]{0:T(1024)S(1)} %pad_clamp_fusion.4), kind=kCustom, calls=%fused_computation.clone.clone.1 | custom fusion | bytes 6291520 | tf_op jit(solution)/shard_map/while/body/eval_jaxpr/gather | solution.py:52
  88.8 5.5 %fusion.78 = f32[16,128,768]{2,1,0:T(8,128)} fusion(bf16[16,128,768]{2,1,0:T(8,128)(2,1)} %gather_fusion, bf16[2,16,128,128]{3,2,1,0:T(8,128)(2,1)S(1)} %get-tuple-element.294, s32[]{:T(128)} %get-tuple-element.280), kind=kOutput, calls=%fused_computation.7.clone.1 | convolution fusion | flops 402653184 | bytes 9961476 | tf_op jit(solution)/shard_map/while/body/eval_jaxpr/kpa,kaf->kpf/dot_general | solution.py:53
  94.3 11.4 %select_add_fusion.4 = f32[8,128,768]{2,0,1:T(8,128)} fusion(f32[8,128,768]{2,0,1:T(8,128)} %get-tuple-element.281, f32[16,128,768]{2,1,0:T(8,128)} %fusion.78, pred[]{:T(512)S(6)} %compare.6, f32[16]{0:T(128)S(1)} %fusion.79, s32[16]{0:T(128)S(1)} %fusion.80), kind=kOutput, calls=%fused_computation.6.clone.1 | convolution fusion | flops 152568064 | bytes 12583041 | tf_op jit(solution)/shard_map/while/body/eval_jaxpr/kr,kpf->rpf/dot_general | solution.py:58
  105.7 4.6 %copy.12 = f32[8,128,768]{2,1,0:T(8,128)} copy(f32[8,128,768]{2,0,1:T(8,128)} %get-tuple-element.91) | data formatting | bytes 6291456 | tf_op jit(solution)/shard_map/while | solution.py:63
  110.3 0.0 reduce-scatter.3.cloned.1.call-update
  110.3 0.0 all-gather.5.cloned.1.call-start
  110.3 36.3 %reduce-scatter.3.cloned.1.call-done = f32[256,768]{1,0:T(8,128)} async-done(((f32[1024,768]{1,0:T(8,128)}), f32[256,768]{1,0:T(8,128)}) %reduce-scatter.3.cloned.1.call-update) | async-done | bytes 786448 | tf_op jit(solution)/shard_map/reduce_scatter | solution.py:65
  146.7 0.0 copy-done
  146.7 1.6 fusion.44
  148.3 0.0 copy-start.2
  148.3 2.6 convolution_convert_fusion.2
  151.0 0.0 all-gather.5.cloned.1.call-update
  151.0 0.2 reduce-scatter.5.cloned.1.call-start
  151.2 19.5 %all-gather.5.cloned.1.call-done = bf16[1024,768]{1,0:T(8,128)(2,1)} async-done(((bf16[256,768]{1,0:T(8,128)(2,1)}), bf16[1024,768]{1,0:T(8,128)(2,1)}) %all-gather.5.cloned.1.call-update) | async-done | bytes 1572880 | tf_op jit(solution)/shard_map/all_gather | solution.py:68
  170.8 41.2 %while.23 = (s32[]{:T(128)}, f32[8,128,768]{2,0,1:T(8,128)}, s32[2,16]{1,0:T(2,128)S(1)}, f32[2,16]{1,0:T(2,128)S(1)}, bf16[2,16,128,128]{3,2,1,0:T(8,128)(2,1)S...) while((s32[]{:T(128)}, f32[8,128,768]{2,0,1:T(8,128)}, ...), condition=%wide.region_4.5_spmd.clone, body=%wide.region_3.4_spmd.clone.sunk | while | flops 555222336 | bytes 28840696 | solution.py:85
  170.8 3.8 %gather_fusion.1 = bf16[16,128,768]{2,1,0:T(8,128)(2,1)} fusion(bf16[8,128,768]{2,1,0:T(8,128)(2,1)} %get-tuple-element.324, s32[1024]{0:T(1024)S(1)} %pad_clamp_fusion.5), kind=kCustom, calls=%fused_computation.1.clone.clone.1 | custom fusion | bytes 6291520 | tf_op jit(solution)/shard_map/while/body/eval_jaxpr/gather | solution.py:74
  174.6 5.6 %fusion.86 = f32[16,128,768]{2,1,0:T(8,128)} fusion(bf16[16,128,768]{2,1,0:T(8,128)(2,1)} %gather_fusion.1, bf16[2,16,128,128]{3,2,1,0:T(8,128)(2,1)S(1)} %get-tuple-element.322, s32[]{:T(128)} %get-tuple-element.309), kind=kOutput, calls=%fused_computation.32.clone.1 | convolution fusion | flops 402653184 | bytes 9961476 | tf_op jit(solution)/shard_map/while/body/eval_jaxpr/kpa,kpf->kaf/dot_general | solution.py:75
  180.2 11.0 %select_add_fusion.5 = f32[8,128,768]{2,0,1:T(8,128)} fusion(f32[8,128,768]{2,0,1:T(8,128)} %get-tuple-element.310, f32[16,128,768]{2,1,0:T(8,128)} %fusion.86, pred[]{:T(512)S(6)} %compare.7, f32[16]{0:T(128)S(1)} %fusion.87, s32[16]{0:T(128)S(1)} %fusion.88), kind=kOutput, calls=%fused_computation.31.clone.1 | convolution fusion | flops 152568064 | bytes 12583041 | tf_op jit(solution)/shard_map/while/body/eval_jaxpr/kc,kaf->caf/dot_general | solution.py:80
  191.2 3.8 %gather_fusion.1 = bf16[16,128,768]{2,1,0:T(8,128)(2,1)} fusion(bf16[8,128,768]{2,1,0:T(8,128)(2,1)} %get-tuple-element.324, s32[1024]{0:T(1024)S(1)} %pad_clamp_fusion.5), kind=kCustom, calls=%fused_computation.1.clone.clone.1 | custom fusion | bytes 6291520 | tf_op jit(solution)/shard_map/while/body/eval_jaxpr/gather | solution.py:74
  195.0 5.6 %fusion.86 = f32[16,128,768]{2,1,0:T(8,128)} fusion(bf16[16,128,768]{2,1,0:T(8,128)(2,1)} %gather_fusion.1, bf16[2,16,128,128]{3,2,1,0:T(8,128)(2,1)S(1)} %get-tuple-element.322, s32[]{:T(128)} %get-tuple-element.309), kind=kOutput, calls=%fused_computation.32.clone.1 | convolution fusion | flops 402653184 | bytes 9961476 | tf_op jit(solution)/shard_map/while/body/eval_jaxpr/kpa,kpf->kaf/dot_general | solution.py:75
  200.5 11.4 %select_add_fusion.5 = f32[8,128,768]{2,0,1:T(8,128)} fusion(f32[8,128,768]{2,0,1:T(8,128)} %get-tuple-element.310, f32[16,128,768]{2,1,0:T(8,128)} %fusion.86, pred[]{:T(512)S(6)} %compare.7, f32[16]{0:T(128)S(1)} %fusion.87, s32[16]{0:T(128)S(1)} %fusion.88), kind=kOutput, calls=%fused_computation.31.clone.1 | convolution fusion | flops 152568064 | bytes 12583041 | tf_op jit(solution)/shard_map/while/body/eval_jaxpr/kc,kaf->caf/dot_general | solution.py:80
  212.0 4.6 %copy.13 = f32[8,128,768]{2,1,0:T(8,128)} copy(f32[8,128,768]{2,0,1:T(8,128)} %get-tuple-element.92) | data formatting | bytes 6291456 | tf_op jit(solution)/shard_map/while | solution.py:85
  216.5 0.0 reduce-scatter.5.cloned.1.call-update
  216.5 74.7 %reduce-scatter.5.cloned.1.call-done = f32[128,768]{1,0:T(8,128)} async-done(((f32[1024,768]{1,0:T(8,128)}), f32[128,768]{1,0:T(8,128)}) %reduce-scatter.5.cloned.1.call-update) | async-done | bytes 393232 | tf_op jit(solution)/shard_map/reduce_scatter | solution.py:86
  291.2 1.7 convert_element_type.24
  (24 shorter events, 0.1 us)
Async XLA Ops:
  7.2 139.5 %copy-start = (bf16[768,768]{1,0:T(8,128)(2,1)S(1)}, bf16[768,768]{1,0:T(8,128)(2,1)}, u32[]{:S(2)}) copy-start(bf16[768,768]{1,0:T(8,128)(2,1)} %param.16) | copy-start | bytes 3538948
  7.2 49.9 %all-gather.3.cloned.1.call-start = ((), (), s32[]{:S(2)}) async-start(), calls=%async_computation.2 | async-start | bytes 1769472 | tf_op jit(solution)/shard_map/all_gather | solution.py:37
  7.9 138.8 %reduce-scatter.3.cloned.1.call-start = ((), (), s32[]{:S(2)}) async-start(), calls=%async_computation.3 | async-start | bytes 3932160 | tf_op jit(solution)/shard_map/reduce_scatter | solution.py:65
  57.1 3.3 %copy-start.4 = (bf16[2,768,768]{2,1,0:T(8,128)(2,1)S(1)}, bf16[2,768,768]{2,1,0:T(8,128)(2,1)}, u32[]{:S(2)}) copy-start(bf16[2,768,768]{2,1,0:T(8,128)(2,1)} %param.17) | copy-start | bytes 7077892
  57.1 3.3 %copy-start.5 = (bf16[1024,768]{1,0:T(8,128)(2,1)S(1)}, bf16[1024,768]{1,0:T(8,128)(2,1)}, u32[]{:S(2)}) copy-start(bf16[1024,768]{1,0:T(8,128)(2,1)} %all-gather.3.cloned.1.call-done) | copy-start | bytes 4718596
  61.8 2.0 copy-start.1
  110.3 36.4 %copy-start.3 = (bf16[256,768]{1,0:T(8,128)(2,1)S(1)}, bf16[256,768]{1,0:T(8,128)(2,1)}, u32[]{:S(2)}) copy-start(bf16[256,768]{1,0:T(8,128)(2,1)} %param.14) | copy-start | bytes 1179652
  110.3 60.5 %all-gather.5.cloned.1.call-start = ((), (), s32[]{:S(2)}) async-start(), calls=%async_computation.4 | async-start | bytes 1966080 | tf_op jit(solution)/shard_map/all_gather | solution.py:68
  148.3 22.5 %copy-start.2 = (bf16[256,768]{1,0:T(8,128)(2,1)}, bf16[256,768]{1,0:T(8,128)(2,1)S(1)}, u32[]{:S(2)}) copy-start(bf16[256,768]{1,0:T(8,128)(2,1)S(1)} %fusion.44) | copy-start | bytes 1179652
  151.0 140.3 %reduce-scatter.5.cloned.1.call-start = ((), (), s32[]{:S(2)}) async-start(), calls=%async_computation.5 | async-start | bytes 3538944 | tf_op jit(solution)/shard_map/reduce_scatter | solution.py:86
Sparse Core Ops, SparseCore 0:
  10.2 46.8 all-gather.2
  110.4 36.2 reduce-scatter.2
  151.1 19.6 all-gather.4
  216.7 74.5 reduce-scatter.4
where the time goes:
time: 300 us; the launch traced here: 299 us
  waiting for transfers between devices  175 us (58%)
  matrix products  75.7 us (25%)
  local copies, waits for them, and re-layouts  26.1 us (9%)
  between operations  14.5 us (5%)
  other arithmetic  7.68 us (3%)
    reduce_scatter x1, waiting for transfers between devices, per_device(): lax.psum_scatter(author_part.reshape(col_blocks * side, width), 'prow', s...  74.7 us
    all_gather x1, waiting for transfers between devices, per_device(): authors = lax.all_gather(author_x, 'prow', axis=0, tiled=True)  43.8 us
    reduce_scatter x1, waiting for transfers between devices, per_device(): lax.psum_scatter(partial_value, 'pcol', scatter_dimension=0, tiled=True)  36.3 us
    dot_general x2, matrix products, second_hop(): jnp.einsum('kc,kaf->caf', placing, product, precision=lax.Precision.HIGHEST)  22.4 us
    dot_general x2, matrix products, first_hop(): jnp.einsum('kr,kpf->rpf', placing, product, precision=lax.Precision.HIGHEST)  22.3 us
    all_gather x1, waiting for transfers between devices, per_device(): lax.all_gather(outgoing, 'pcol', axis=0, tiled=True)  19.5 us
    dot_general x2, matrix products, second_hop(): jnp.einsum('kpa,kpf->kaf', content_now, picked, preferred_element_type=jn...  11.1 us
    dot_general x2, matrix products, first_hop(): jnp.einsum('kpa,kaf->kpf', content_now, picked, preferred_element_type=jn...  11 us
  transfers between devices with their start and end apart: 4, of which 4 were waited for; matrix products, arithmetic and copies ran while one was open for 2% of the time, Pallas kernels for 0%

commit v1 on v0

--- a/solution.py
+++ b/solution.py
@@ -34,7 +34,9 @@
     )
     contents = block_vals.reshape(groups, GROUP, side, side)
     self_term = jnp.dot(paper_x, w_self, preferred_element_type=jnp.float32)
-    authors = lax.all_gather(author_x, "prow", axis=0, tiled=True)
+    authors = jnp.concatenate(
+        lax.all_to_all(jnp.stack([author_x] * lax.axis_size("prow")), "prow", 0, 0), axis=0
+    )
     messages = jnp.stack(
         [
             jnp.dot(authors, w_rel[index], preferred_element_type=jnp.float32)

time: 300 us -> 297 us (0.990)
  waiting for transfers between devices: 175 us -> 165 us
  starting transfers between devices: 0.34 us -> 7.61 us
    all_gather x1 -> x0, waiting for transfers between devices: 43.8 us -> none  [per_device(): authors = lax.all_gather(author_x, 'prow', axis=0, tiled=True)]
    all_to_all x0 -> x1, waiting for transfers between devices: none -> 33.5 us  [per_device(): lax.all_to_all(jnp.stack([author_x] * lax.axis_size('prow')), 'prow', 0, 0)]
    all_to_all x0 -> x1, starting transfers between devices: none -> 7.31 us  [per_device(): lax.all_to_all(jnp.stack([author_x] * lax.axis_size('prow')), 'prow', 0, 0)]
  transfers between devices with their start and end apart: 4 -> 4, of which waited for: 4 -> 4; matrix products, arithmetic and copies ran while one was open for 2% -> 1% of each run, Pallas kernels for 0% -> 0%
where the time goes in v1:
time: 297 us; the launch traced here: 296 us
  waiting for transfers between devices  165 us (56%)
  matrix products  75.3 us (25%)
  local copies, waits for them, and re-layouts  28.4 us (10%)
  between operations  14.5 us (5%)
  starting transfers between devices  7.61 us (3%)
  other arithmetic  5.73 us (2%)
    reduce_scatter x1, waiting for transfers between devices, per_device(): lax.psum_scatter(author_part.reshape(col_blocks * side, width), 'prow', s...  74.5 us
    reduce_scatter x1, waiting for transfers between devices, per_device(): lax.psum_scatter(partial_value, 'pcol', scatter_dimension=0, tiled=True)  37 us
    all_to_all x1, waiting for transfers between devices, per_device(): lax.all_to_all(jnp.stack([author_x] * lax.axis_size('prow')), 'prow', 0, 0)  33.5 us
    dot_general x2, matrix products, second_hop(): jnp.einsum('kc,kaf->caf', placing, product, precision=lax.Precision.HIGHEST)  22.4 us
    dot_general x2, matrix products, first_hop(): jnp.einsum('kr,kpf->rpf', placing, product, precision=lax.Precision.HIGHEST)  22.3 us
    all_gather x1, waiting for transfers between devices, per_device(): lax.all_gather(outgoing, 'pcol', axis=0, tiled=True)  19.5 us
    dot_general x2, matrix products, second_hop(): jnp.einsum('kpa,kpf->kaf', content_now, picked, preferred_element_type=jn...  11.2 us
    dot_general x2, matrix products, first_hop(): jnp.einsum('kpa,kaf->kpf', content_now, picked, preferred_element_type=jn...  11 us
  transfers between devices with their start and end apart: 4, of which 4 were waited for; matrix products, arithmetic and copies ran while one was open for 1% of the time, Pallas kernels for 0%

profile of v1, /device:TPU:0, one launch (start us, length us, event | category | flops | bytes accessed | tf_op | source)
XLA Modules:
  0.0 296.3 jit_solution(11222777386300679066)
XLA Ops:
  7.2 0.0 copy-start
  7.2 0.0 copy-start.5
  7.2 0.0 copy-start.6
  7.2 0.0 copy-start.7
  7.2 2.3 stack.11
  9.5 7.3 %all-to-all-start = ((bf16[8,128,768]{2,1,0:T(8,128)(2,1)}), bf16[8,128,768]{2,1,0:T(8,128)(2,1)S(1)}, u32[]{:S(2)}, u32[]{:S(2)}) async-start(bf16[8,128,768]{2,1,0:T(8,128)(2,1)} %stack.11), calls=%async_computation | async-start | bytes 3145728 | tf_op jit(solution)/shard_map/all_to_all | solution.py:38
  16.8 0.0 reduce-scatter.3.cloned.1.call-start
  16.8 0.5 broadcast.118
  17.4 0.7 reduce.9
  18.0 0.1 reshape.108
  18.1 0.7 reduce.11
  18.8 0.1 reshape.112
  18.9 0.7 reduce.10
  19.5 0.1 reshape.111
  20.3 33.5 %all-to-all-done = bf16[8,128,768]{2,1,0:T(8,128)(2,1)S(1)} async-done(((bf16[8,128,768]{2,1,0:T(8,128)(2,1)}), bf16[8,128,768]{2,1,0:T(8,128)(2,1)S(1)}, u32[]{:S(2)}, u32[]{:S(2)}) %all-to-all-start) | async-done | bytes 1572896 | tf_op jit(solution)/shard_map/all_to_all | solution.py:38
  53.8 2.8 fusion.41
  56.6 1.4 fusion.42
  58.0 0.0 copy-start.1
  58.0 2.0 pad_maximum_fusion
  60.0 0.0 copy-done.1
  60.0 42.0 %while.22 = (s32[]{:T(128)}, f32[8,128,768]{2,0,1:T(8,128)}, s32[2,16]{1,0:T(2,128)S(1)}, f32[2,16]{1,0:T(2,128)S(1)}, bf16[2,16,128,128]{3,2,1,0:T(8,128)(2,1)S...) while((s32[]{:T(128)}, f32[8,128,768]{2,0,1:T(8,128)}, ...), condition=%wide.region_1.2_spmd.clone, body=%wide.region_0.1_spmd.clone.sunk | while | flops 555222400 | bytes 28840768 | solution.py:65
  60.0 4.3 %gather_fusion = bf16[16,128,768]{2,1,0:T(8,128)(2,1)} fusion(bf16[16,128,768]{2,1,0:T(8,128)(2,1)} %get-tuple-element.297, s32[1024]{0:T(1024)S(1)} %pad_clamp_fusion.4), kind=kCustom, calls=%fused_computation.clone.clone.1 | custom fusion | bytes 6291520 | tf_op jit(solution)/shard_map/while/body/eval_jaxpr/gather | solution.py:54
  64.3 5.5 %fusion.78 = f32[16,128,768]{2,1,0:T(8,128)} fusion(bf16[16,128,768]{2,1,0:T(8,128)(2,1)} %gather_fusion, bf16[2,16,128,128]{3,2,1,0:T(8,128)(2,1)S(1)} %get-tuple-element.294, s32[]{:T(128)} %get-tuple-element.280), kind=kOutput, calls=%fused_computation.7.clone.1 | convolution fusion | flops 402653184 | bytes 9961476 | tf_op jit(solution)/shard_map/while/body/eval_jaxpr/kpa,kaf->kpf/dot_general | solution.py:55
  69.9 10.9 %select_add_fusion.4 = f32[8,128,768]{2,0,1:T(8,128)} fusion(f32[8,128,768]{2,0,1:T(8,128)} %get-tuple-element.281, f32[16,128,768]{2,1,0:T(8,128)} %fusion.78, pred[]{:T(512)S(6)} %compare.6, f32[16]{0:T(128)S(1)} %fusion.79, s32[16]{0:T(128)S(1)} %fusion.80), kind=kOutput, calls=%fused_computation.6.clone.1 | convolution fusion | flops 152568064 | bytes 12583041 | tf_op jit(solution)/shard_map/while/body/eval_jaxpr/kr,kpf->rpf/dot_general | solution.py:60
  80.8 4.3 %gather_fusion = bf16[16,128,768]{2,1,0:T(8,128)(2,1)} fusion(bf16[16,128,768]{2,1,0:T(8,128)(2,1)} %get-tuple-element.297, s32[1024]{0:T(1024)S(1)} %pad_clamp_fusion.4), kind=kCustom, calls=%fused_computation.clone.clone.1 | custom fusion | bytes 6291520 | tf_op jit(solution)/shard_map/while/body/eval_jaxpr/gather | solution.py:54
  85.1 5.5 %fusion.78 = f32[16,128,768]{2,1,0:T(8,128)} fusion(bf16[16,128,768]{2,1,0:T(8,128)(2,1)} %gather_fusion, bf16[2,16,128,128]{3,2,1,0:T(8,128)(2,1)S(1)} %get-tuple-element.294, s32[]{:T(128)} %get-tuple-element.280), kind=kOutput, calls=%fused_computation.7.clone.1 | convolution fusion | flops 402653184 | bytes 9961476 | tf_op jit(solution)/shard_map/while/body/eval_jaxpr/kpa,kaf->kpf/dot_general | solution.py:55
  90.6 11.4 %select_add_fusion.4 = f32[8,128,768]{2,0,1:T(8,128)} fusion(f32[8,128,768]{2,0,1:T(8,128)} %get-tuple-element.281, f32[16,128,768]{2,1,0:T(8,128)} %fusion.78, pred[]{:T(512)S(6)} %compare.6, f32[16]{0:T(128)S(1)} %fusion.79, s32[16]{0:T(128)S(1)} %fusion.80), kind=kOutput, calls=%fused_computation.6.clone.1 | convolution fusion | flops 152568064 | bytes 12583041 | tf_op jit(solution)/shard_map/while/body/eval_jaxpr/kr,kpf->rpf/dot_general | solution.py:60
  102.0 4.6 %copy.12 = f32[8,128,768]{2,1,0:T(8,128)} copy(f32[8,128,768]{2,0,1:T(8,128)} %get-tuple-element.91) | data formatting | bytes 6291456 | tf_op jit(solution)/shard_map/while | solution.py:65
  106.6 0.0 reduce-scatter.3.cloned.1.call-update
  106.6 0.0 all-gather.2.cloned.1.call-start
  106.6 37.0 %reduce-scatter.3.cloned.1.call-done = f32[256,768]{1,0:T(8,128)} async-done(((f32[1024,768]{1,0:T(8,128)}), f32[256,768]{1,0:T(8,128)}) %reduce-scatter.3.cloned.1.call-update) | async-done | bytes 786448 | tf_op jit(solution)/shard_map/reduce_scatter | solution.py:67
  143.7 1.6 fusion.44
  145.3 0.0 copy-start.2
  145.3 2.6 convolution_convert_fusion.2
  148.0 0.0 all-gather.2.cloned.1.call-update
  148.0 0.2 reduce-scatter.5.cloned.1.call-start
  148.2 19.5 %all-gather.2.cloned.1.call-done = bf16[1024,768]{1,0:T(8,128)(2,1)} async-done(((bf16[256,768]{1,0:T(8,128)(2,1)}), bf16[1024,768]{1,0:T(8,128)(2,1)}) %all-gather.2.cloned.1.call-update) | async-done | bytes 1572880 | tf_op jit(solution)/shard_map/all_gather | solution.py:70
  167.8 41.3 %while.23 = (s32[]{:T(128)}, f32[8,128,768]{2,0,1:T(8,128)}, s32[2,16]{1,0:T(2,128)S(1)}, f32[2,16]{1,0:T(2,128)S(1)}, bf16[2,16,128,128]{3,2,1,0:T(8,128)(2,1)S...) while((s32[]{:T(128)}, f32[8,128,768]{2,0,1:T(8,128)}, ...), condition=%wide.region_4.5_spmd.clone, body=%wide.region_3.4_spmd.clone.sunk | while | flops 555222336 | bytes 28840696 | solution.py:87
  167.8 3.8 %gather_fusion.1 = bf16[16,128,768]{2,1,0:T(8,128)(2,1)} fusion(bf16[8,128,768]{2,1,0:T(8,128)(2,1)} %get-tuple-element.324, s32[1024]{0:T(1024)S(1)} %pad_clamp_fusion.5), kind=kCustom, calls=%fused_computation.1.clone.clone.1 | custom fusion | bytes 6291520 | tf_op jit(solution)/shard_map/while/body/eval_jaxpr/gather | solution.py:76
  171.6 5.6 %fusion.86 = f32[16,128,768]{2,1,0:T(8,128)} fusion(bf16[16,128,768]{2,1,0:T(8,128)(2,1)} %gather_fusion.1, bf16[2,16,128,128]{3,2,1,0:T(8,128)(2,1)S(1)} %get-tuple-element.322, s32[]{:T(128)} %get-tuple-element.309), kind=kOutput, calls=%fused_computation.32.clone.1 | convolution fusion | flops 402653184 | bytes 9961476 | tf_op jit(solution)/shard_map/while/body/eval_jaxpr/kpa,kpf->kaf/dot_general | solution.py:77
  177.2 11.0 %select_add_fusion.5 = f32[8,128,768]{2,0,1:T(8,128)} fusion(f32[8,128,768]{2,0,1:T(8,128)} %get-tuple-element.310, f32[16,128,768]{2,1,0:T(8,128)} %fusion.86, pred[]{:T(512)S(6)} %compare.7, f32[16]{0:T(128)S(1)} %fusion.87, s32[16]{0:T(128)S(1)} %fusion.88), kind=kOutput, calls=%fused_computation.31.clone.1 | convolution fusion | flops 152568064 | bytes 12583041 | tf_op jit(solution)/shard_map/while/body/eval_jaxpr/kc,kaf->caf/dot_general | solution.py:82
  188.2 3.8 %gather_fusion.1 = bf16[16,128,768]{2,1,0:T(8,128)(2,1)} fusion(bf16[8,128,768]{2,1,0:T(8,128)(2,1)} %get-tuple-element.324, s32[1024]{0:T(1024)S(1)} %pad_clamp_fusion.5), kind=kCustom, calls=%fused_computation.1.clone.clone.1 | custom fusion | bytes 6291520 | tf_op jit(solution)/shard_map/while/body/eval_jaxpr/gather | solution.py:76
  192.0 5.6 %fusion.86 = f32[16,128,768]{2,1,0:T(8,128)} fusion(bf16[16,128,768]{2,1,0:T(8,128)(2,1)} %gather_fusion.1, bf16[2,16,128,128]{3,2,1,0:T(8,128)(2,1)S(1)} %get-tuple-element.322, s32[]{:T(128)} %get-tuple-element.309), kind=kOutput, calls=%fused_computation.32.clone.1 | convolution fusion | flops 402653184 | bytes 9961476 | tf_op jit(solution)/shard_map/while/body/eval_jaxpr/kpa,kpf->kaf/dot_general | solution.py:77
  197.6 11.4 %select_add_fusion.5 = f32[8,128,768]{2,0,1:T(8,128)} fusion(f32[8,128,768]{2,0,1:T(8,128)} %get-tuple-element.310, f32[16,128,768]{2,1,0:T(8,128)} %fusion.86, pred[]{:T(512)S(6)} %compare.7, f32[16]{0:T(128)S(1)} %fusion.87, s32[16]{0:T(128)S(1)} %fusion.88), kind=kOutput, calls=%fused_computation.31.clone.1 | convolution fusion | flops 152568064 | bytes 12583041 | tf_op jit(solution)/shard_map/while/body/eval_jaxpr/kc,kaf->caf/dot_general | solution.py:82
  209.0 4.6 %copy.13 = f32[8,128,768]{2,1,0:T(8,128)} copy(f32[8,128,768]{2,0,1:T(8,128)} %get-tuple-element.92) | data formatting | bytes 6291456 | tf_op jit(solution)/shard_map/while | solution.py:87
  213.6 0.0 reduce-scatter.5.cloned.1.call-update
  213.6 74.5 %reduce-scatter.5.cloned.1.call-done = f32[128,768]{1,0:T(8,128)} async-done(((f32[1024,768]{1,0:T(8,128)}), f32[128,768]{1,0:T(8,128)}) %reduce-scatter.5.cloned.1.call-update) | async-done | bytes 393232 | tf_op jit(solution)/shard_map/reduce_scatter | solution.py:88
  288.1 1.7 convert_element_type.24
  (28 shorter events, 0.1 us)
Async XLA Ops:
  7.2 136.5 %copy-start = (bf16[768,768]{1,0:T(8,128)(2,1)S(1)}, bf16[768,768]{1,0:T(8,128)(2,1)}, u32[]{:S(2)}) copy-start(bf16[768,768]{1,0:T(8,128)(2,1)} %param.16) | copy-start | bytes 3538948
  7.2 10.2 %copy-start.5 = (s32[1,1,32]{2,1,0:T(1,128)S(1)}, s32[1,1,32]{2,1,0:T(1,128)}, u32[]{:S(2)}) copy-start(s32[1,1,32]{2,1,0:T(1,128)} %param.19) | copy-start | bytes 388
  7.2 10.9 %copy-start.6 = (s32[1,1,32]{2,1,0:T(1,128)S(1)}, s32[1,1,32]{2,1,0:T(1,128)}, u32[]{:S(2)}) copy-start(s32[1,1,32]{2,1,0:T(1,128)} %param.20) | copy-start | bytes 388
  7.2 11.7 %copy-start.7 = (s32[1,1,32]{2,1,0:T(1,128)S(1)}, s32[1,1,32]{2,1,0:T(1,128)}, u32[]{:S(2)}) copy-start(s32[1,1,32]{2,1,0:T(1,128)} %param.21) | copy-start | bytes 388
  9.5 44.3 %all-to-all-start = ((bf16[8,128,768]{2,1,0:T(8,128)(2,1)}), bf16[8,128,768]{2,1,0:T(8,128)(2,1)S(1)}, u32[]{:S(2)}, u32[]{:S(2)}) async-start(bf16[8,128,768]{2,1,0:T(8,128)(2,1)} %stack.11), calls=%async_computation | async-start | bytes 3145728 | tf_op jit(solution)/shard_map/all_to_all | solution.py:38
  16.8 126.9 %reduce-scatter.3.cloned.1.call-start = ((), (), s32[]{:S(2)}) async-start(), calls=%async_computation.3 | async-start | bytes 3932160 | tf_op jit(solution)/shard_map/reduce_scatter | solution.py:67
  53.8 2.8 copy-start.4
  58.0 2.0 copy-start.1
  106.6 37.1 %copy-start.3 = (bf16[256,768]{1,0:T(8,128)(2,1)S(1)}, bf16[256,768]{1,0:T(8,128)(2,1)}, u32[]{:S(2)}) copy-start(bf16[256,768]{1,0:T(8,128)(2,1)} %param.14) | copy-start | bytes 1179652
  106.6 61.2 %all-gather.2.cloned.1.call-start = ((), (), s32[]{:S(2)}) async-start(), calls=%async_computation.4 | async-start | bytes 1966080 | tf_op jit(solution)/shard_map/all_gather | solution.py:70
  145.3 22.5 %copy-start.2 = (bf16[256,768]{1,0:T(8,128)(2,1)}, bf16[256,768]{1,0:T(8,128)(2,1)S(1)}, u32[]{:S(2)}) copy-start(bf16[256,768]{1,0:T(8,128)(2,1)S(1)} %fusion.44) | copy-start | bytes 1179652
  148.0 140.1 %reduce-scatter.5.cloned.1.call-start = ((), (), s32[]{:S(2)}) async-start(), calls=%async_computation.5 | async-start | bytes 3538944 | tf_op jit(solution)/shard_map/reduce_scatter | solution.py:88
Sparse Core Ops, SparseCore 0:
  106.7 36.9 reduce-scatter.2
  148.1 19.6 all-gather.1
  213.7 74.3 reduce-scatter.4
